TPU v7x, 32 devices: a whole 2x2x4 slice. The times are simulated.
32 devices in a mesh: groups: 2 (over y), dp: 4 (over z), tgt: 4 (over x, core).
Axes of the slice: x: 2, y: 2, z: 4, core: 2. Of those that a mesh axis runs over, the one named last changes fastest.
Arguments:
- hidden: bfloat16 [6144, 4096], P(('groups', 'dp', 'tgt')), parts along dimension 0, may hold values from -6 to 6
- cotangent: bfloat16 [6144, 4096], P(('groups', 'dp', 'tgt')), parts along dimension 0, may hold values from -6 to 6
- adapter_down_weight: bfloat16 [4096, 64], replicated, may hold values from -0.09375 to 0.09375
- adapter_up_weight: bfloat16 [64, 4096], replicated, may hold values from -0.75 to 0.75
- width_projection_factor: bfloat16 [4096, 512], replicated, may hold values from -0.09375 to 0.09375
- rank_projection_factor: bfloat16 [64, 8], replicated, may hold values from -0.75 to 0.75
- targets: bfloat16 [8, 768, 8192], P(('groups', 'dp'), 'tgt'), parts along dimension 0, may hold values from -100 to 100
- strata: int32 [768], P(('groups', 'dp', 'tgt')), parts along dimension 0, may hold values from 0 to 31
- keep: int32 [768], P(('groups', 'dp', 'tgt')), parts along dimension 0, may hold values from 0 to 1
- shard_example_count: int32 [32], P(('groups', 'dp', 'tgt')), parts along dimension 0, may hold values from 18 to 24
- stratum_owner_table: int32 [32], replicated, may hold values from 0 to 3, as said below
Outputs:
- selection: float32 [768], P(('groups', 'dp', 'tgt')), parts along dimension 0
There are 2 independent parts, one for each index of `groups`. A program takes and returns all parts, laid end to end along the dimension named above; an argument that names none is the same for every part. Nothing has to cross between parts.
Inputs may be any that keep to these rules, and one draw needn't show every extreme that they name: `stratum_owner_table`: each of the 4 owners holds exactly 8 strata.
All inputs are finite; a program needn't handle non-finite values.
Results may differ from a plain program's by a relative error of at most 0.0029.
Values may be sent and summed in bfloat16 or wider, within the bound.
A program may use at most 64 MiB of HBM per device.

v0:
```python
import math
import jax
import jax.numpy as jnp
from jax import lax
from jax.sharding import PartitionSpec as P

FEAT = 8192
CAP = 2
TGT = 768
TASKS = 16
epsilon = 1e-06


def contracted_row_sums(row_block, col_block):
    return lax.dot_general(
        row_block, col_block, (((1,), (1,)), ((), ())), preferred_element_type=jnp.float32
    )


def inverse_norms(values):
    widened = values.astype(jnp.float32)
    return lax.rsqrt(jnp.sum(widened * widened, axis=1) + epsilon)


def task_terms(row_block, row_inv, col_block, col_inv, first_index):
    per_task = TGT // TASKS
    products = contracted_row_sums(row_block, col_block)
    aligned = math.sqrt(FEAT) * products * row_inv[:, None] * col_inv[None, :]
    target_ids = (first_index + jnp.arange(col_block.shape[0], dtype=jnp.int32)) // per_task
    task_mask = (target_ids[:, None] == jnp.arange(TASKS, dtype=jnp.int32)[None, :]).astype(
        jnp.float32
    )
    return jnp.dot(jnp.maximum(aligned, 0.0), task_mask, precision=lax.Precision.HIGHEST)


def per_example(values, examples):
    return values.reshape(examples, -1, values.shape[1])


def shards(
    hidden,
    cotangent,
    adapter_down_weight,
    adapter_up_weight,
    width_projection_factor,
    rank_projection_factor,
    targets,
    strata,
    keep,
    shard_example_count,
    stratum_owner_table,
):
    examples = strata.shape[0]
    strata_total = stratum_owner_table.shape[0]
    ordinal = jnp.arange(examples, dtype=jnp.int32)
    usable = ordinal < shard_example_count[0]
    is_live = jnp.logical_and(keep == 1, usable)
    member = strata[:, None] == jnp.arange(strata_total, dtype=jnp.int32)[None, :]
    local_counts = jnp.sum(jnp.logical_and(member, is_live[:, None]).astype(jnp.float32), axis=0)
    counts = lax.psum(local_counts, ("dp", "tgt"))
    down_activation = jnp.dot(
        hidden, adapter_down_weight, preferred_element_type=jnp.float32
    ).astype(jnp.bfloat16)
    up_backward_product = contracted_row_sums(cotangent, adapter_up_weight).astype(jnp.bfloat16)
    wide_hidden = jnp.dot(
        hidden, width_projection_factor, preferred_element_type=jnp.float32
    ).astype(jnp.bfloat16)
    wide_back = jnp.dot(
        cotangent, width_projection_factor, preferred_element_type=jnp.float32
    ).astype(jnp.bfloat16)
    rank_down = jnp.dot(
        down_activation, rank_projection_factor, preferred_element_type=jnp.float32
    ).astype(jnp.bfloat16)
    rank_up = jnp.dot(
        up_backward_product, rank_projection_factor, preferred_element_type=jnp.float32
    ).astype(jnp.bfloat16)
    up_grad = jnp.einsum(
        "esr,esd->erd",
        per_example(rank_down, examples),
        per_example(wide_back, examples),
        preferred_element_type=jnp.float32,
    )
    down_grad = jnp.einsum(
        "esd,esr->edr",
        per_example(wide_hidden, examples),
        per_example(rank_up, examples),
        preferred_element_type=jnp.float32,
    )
    features = jnp.concatenate(
        [up_grad.reshape(examples, -1), down_grad.reshape(examples, -1)], axis=1
    ).astype(jnp.bfloat16)
    owner_of = jnp.sum(jnp.where(member, stratum_owner_table[None, :], 0), axis=1)
    earlier = ordinal[:, None] > ordinal[None, :]
    same_owner = owner_of[:, None] == owner_of[None, :]
    ahead = jnp.logical_and(jnp.logical_and(earlier, same_owner), is_live[None, :])
    slot_rank = jnp.sum(ahead.astype(jnp.int32), axis=1)
    is_sent = jnp.logical_and(is_live, slot_rank < CAP)
    owner_count = lax.axis_size("dp")
    slot_index = owner_of * CAP + slot_rank
    slot_ids = jnp.arange(owner_count * CAP, dtype=jnp.int32)
    dispatch = jnp.logical_and(slot_ids[:, None] == slot_index[None, :], is_sent[None, :])
    outgoing = jnp.dot(
        dispatch.astype(jnp.bfloat16), features, preferred_element_type=jnp.float32
    ).astype(jnp.bfloat16)
    received = lax.all_to_all(
        outgoing.reshape(owner_count, CAP, -1), "dp", split_axis=0, concat_axis=0, tiled=True
    )
    owner_rows = received.reshape(owner_count * CAP, -1)
    own_targets = targets[0]
    target_inv = inverse_norms(own_targets)
    offset = lax.axis_index("tgt") * own_targets.shape[0]
    row_piece = lax.all_gather(owner_rows, "tgt", axis=0, tiled=True)
    partials = task_terms(row_piece, inverse_norms(row_piece), own_targets, target_inv, offset)
    task_sums = lax.psum_scatter(partials, "tgt", scatter_dimension=0, tiled=True)
    raw_owner = jnp.max(task_sums / (TGT // TASKS), axis=1)
    returned = lax.all_to_all(
        raw_owner.reshape(owner_count, CAP), "dp", split_axis=0, concat_axis=0, tiled=True
    ).reshape(owner_count * CAP)
    raw_score = jnp.sum(jnp.where(dispatch, returned[:, None], 0.0), axis=0)
    stratum_count = jnp.sum(jnp.where(member, counts[None, :], 0.0), axis=1)
    weight = jnp.sqrt(jnp.sum(counts) / (strata_total * jnp.maximum(stratum_count, 1.0)))
    return jnp.where(is_sent, raw_score * weight, 0.0)


def solution(mesh):
    return jax.shard_map(
        shards,
        mesh=mesh,
        in_specs=(
            P(("groups", "dp", "tgt"), None),
            P(("groups", "dp", "tgt"), None),
            P(),
            P(),
            P(),
            P(),
            P(("groups", "dp"), "tgt", None),
            P(("groups", "dp", "tgt")),
            P(("groups", "dp", "tgt")),
            P(("groups", "dp", "tgt")),
            P(),
        ),
        out_specs=P(("groups", "dp", "tgt")),
        check_vma=False,
    )
```

profile of v0, /device:TPU:0, one launch (start us, length us, event | category | flops | bytes accessed | tf_op | source)
XLA Modules:
  0.0 93.7 jit_solution(1229232755631329175)
XLA Ops:
  0.8 0.7 compare_and_fusion.1
  1.4 0.9 select_reduce_fusion.1
  2.3 0.2 convert_reduce_fusion.1
  2.5 0.7 compare_and_fusion
  3.2 2.3 %fusion.15 = bf16[192,8]{0,1:T(8,128)(2,1)S(1)} fusion(bf16[64,8]{0,1:T(8,128)(2,1)} %param.16, bf16[192,4096]{1,0:T(8,128)(2,1)} %param.12, bf16[64,4096]{1,0:T(8,128)(2,1)} %param.14), kind=kOutput, calls=%fused_computation.17 | convolution fusion | flops 100873728 | bytes 2101248 | tf_op jit(solution)/shard_map/dot_general | solution.py:74
  5.5 0.1 reshape.70
  5.6 3.3 %convolution_convert_fusion.1 = bf16[24,512,8]{1,2,0:T(8,128)(2,1)S(1)} fusion(bf16[192,4096]{1,0:T(8,128)(2,1)S(1)} %copy-done, bf16[4096,512]{1,0:T(8,128)(2,1)} %param.15, bf16[24,8,8]{1,0,2:T(8,128)(2,1)S(1)} %reshape.70), kind=kOutput, calls=%fused_computation.4 | convolution fusion | flops 807075840 | bytes 5966848 | tf_op jit(solution)/shard_map/esd,esr->edr/dot_general | solution.py:83
  8.9 0.8 copy.25
  9.8 0.3 copy.26
  10.1 1.9 %fusion.16 = bf16[192,8]{0,1:T(8,128)(2,1)S(1)} fusion(bf16[64,8]{0,1:T(8,128)(2,1)S(1)} %copy-done.2, bf16[192,4096]{1,0:T(8,128)(2,1)S(1)} %copy-done, bf16[4096,64]{0,1:T(8,128)(2,1)} %param.13), kind=kOutput, calls=%fused_computation.18 | convolution fusion | flops 100873728 | bytes 2101248 | tf_op jit(solution)/shard_map/dot_general | solution.py:71
  12.0 0.7 reshape.66
  12.8 3.3 %convolution_convert_fusion.3 = bf16[24,8,512]{2,1,0:T(8,128)(2,1)S(1)} fusion(bf16[192,4096]{1,0:T(8,128)(2,1)S(1)} %copy-done.1, bf16[4096,512]{1,0:T(8,128)(2,1)} %param.15, bf16[24,8,8]{1,0,2:T(8,128)(2,1)} %reshape.66), kind=kOutput, calls=%fused_computation.6 | convolution fusion | flops 807075840 | bytes 5966848 | tf_op jit(solution)/shard_map/esr,esd->erd/dot_general | solution.py:77
  16.2 0.2 convolution_convert_fusion
  16.4 0.7 reshape.72
  17.1 6.3 %all-to-all-start = ((bf16[4,2,8192]{2,1,0:T(2,128)(2,1)}), bf16[4,2,8192]{2,1,0:T(2,128)(2,1)S(1)}, u32[]{:S(2)}, u32[]{:S(2)}) async-start(bf16[4,2,8192]{2,1,0:T(2,128)(2,1)} %reshape.72), calls=%async_computation | async-start | bytes 262144 | tf_op jit(solution)/shard_map/all_to_all | solution.py:105
  23.5 0.7 convert_reduce_fusion
  24.2 2.6 %multiply_reduce_fusion = f32[192]{0:T(256)S(1)} fusion(bf16[1,192,8192]{2,1,0:T(8,128)(2,1)} %param.17), kind=kLoop, calls=%fused_computation.1 | loop fusion | flops 4718400 | bytes 3146496 | tf_op jit(solution)/shard_map/reduce_sum | solution.py:22
  26.9 33.1 %psum.7 = f32[32]{0:T(128)S(1)} all-reduce(f32[32]{0:T(128)S(1)} %convert_reduce_fusion), channel_id=1, replica_groups=mesh['groups'=2,'dp'=4,'tgt'=4] {'dp','tgt'}, use_global_device_ids=true, to_apply=%region_8.9 | all-reduce | flops 32 | bytes 256 | tf_op jit(solution)/shard_map/psum | solution.py:60
  60.0 0.2 select_reduce_fusion
  60.2 0.6 reduce_sum.78
  60.8 0.6 dynamic-slice
  62.1 6.5 %all_gather.3 = bf16[32,8192]{1,0:T(8,128)(2,1)S(1)} all-gather(bf16[8,8192]{1,0:T(8,128)(2,1)S(1)} %reshape.73), channel_id=1, replica_groups=mesh['groups'=2,'dp'=4,'tgt'=4] {'tgt'}, dimensions={0}, use_global_device_ids=true | all-gather | bytes 655360 | tf_op jit(solution)/shard_map/all_gather | solution.py:112
  68.6 0.2 multiply_reduce_fusion.1
  68.8 3.0 %fusion.10 = f32[32,192]{1,0:T(8,128)S(1)} fusion(bf16[32,8192]{1,0:T(8,128)(2,1)S(1)} %all_gather.3, bf16[1,192,8192]{2,1,0:T(8,128)(2,1)} %param.17, f32[192]{0:T(256)S(1)} %add_rsqrt_fusion, f32[32]{0:T(128)S(1)} %rsqrt_multiply_fusion), kind=kOutput, calls=%fused_computation.14 | convolution fusion | flops 100681728 | bytes 3695488 | tf_op jit(solution)/shard_map/dot_general | solution.py:15
  71.8 0.2 fusion.20
  72.0 11.1 %all-reduce = f32[32,16]{1,0:T(8,128)S(1)} all-reduce(f32[32,16]{1,0:T(8,128)S(1)} %fusion.20), channel_id=2, replica_groups=mesh['groups'=2,'dp'=4,'tgt'=4] {'tgt'}, use_global_device_ids=true, to_apply=%region_4.5.clone | all-reduce | flops 512 | bytes 4096
  83.2 0.1 fusion.27
  83.4 7.9 %all_to_all.14 = f32[4,1,2]{2,1,0:T(1,128)S(1)} all-to-all(f32[4,1,2]{2,1,0:T(1,128)S(1)} %bitcast.45), channel_id=1, replica_groups=mesh['groups'=2,'dp'=4,'tgt'=4] {'dp'}, dimensions={0} | all-to-all | bytes 64 | tf_op jit(solution)/shard_map/all_to_all | solution.py:116
  91.3 0.5 broadcast.76
  91.8 0.7 reduce.3
  92.6 0.1 select_reduce_fusion.2
  92.6 1.1 %multiply_select_fusion = f32[24]{0:T(128)} fusion(pred[24]{0:T(512)(128)(4,1)S(1)} %compare_and_fusion, f32[24]{0:T(128)S(1)} %select_reduce_fusion.2, f32[24]{0:T(128)S(1)} %select_reduce_fusion, f32[]{:T(128)} %reduce_sum.78), kind=kLoop, calls=%fused_computation.48 | loop fusion | flops 120 | bytes 316 | tf_op jit(solution)/shard_map/jit(_where)/select_n | solution.py:122
  (19 shorter events, 0.4 us)
Async XLA Ops:
  0.0 5.6 %copy-start = (bf16[192,4096]{1,0:T(8,128)(2,1)S(1)}, bf16[192,4096]{1,0:T(8,128)(2,1)}, u32[]{:S(2)}) copy-start(bf16[192,4096]{1,0:T(8,128)(2,1)} %param.11) | copy-start | bytes 4718596
  8.9 1.2 %copy-start.2 = (bf16[64,8]{0,1:T(8,128)(2,1)S(1)}, bf16[64,8]{0,1:T(8,128)(2,1)}, u32[]{:S(2)}) copy-start(bf16[64,8]{0,1:T(8,128)(2,1)} %param.16) | copy-start | bytes 3076
  10.1 2.7 %copy-start.1 = (bf16[192,4096]{1,0:T(8,128)(2,1)S(1)}, bf16[192,4096]{1,0:T(8,128)(2,1)}, u32[]{:S(2)}) copy-start(bf16[192,4096]{1,0:T(8,128)(2,1)} %param.12) | copy-start | bytes 4718596
  17.1 44.9 %all-to-all-start = ((bf16[4,2,8192]{2,1,0:T(2,128)(2,1)}), bf16[4,2,8192]{2,1,0:T(2,128)(2,1)S(1)}, u32[]{:S(2)}, u32[]{:S(2)}) async-start(bf16[4,2,8192]{2,1,0:T(2,128)(2,1)} %reshape.72), calls=%async_computation | async-start | bytes 262144 | tf_op jit(solution)/shard_map/all_to_all | solution.py:105
  24.2 35.8 %copy-start.3 = (s32[24]{0:T(128)S(1)}, s32[24]{0:T(128)}, u32[]{:S(2)}) copy-start(s32[24]{0:T(128)} %param.18) | copy-start | bytes 292
  24.2 36.5 %copy-start.4 = (u32[32]{0:T(128)S(1)}, u32[32]{0:T(128)}, u32[]{:S(2)}) copy-start(u32[32]{0:T(128)} %constant.44) | copy-start | bytes 388
where the time goes:
time: 94.3 us; the launch traced here: 93.7 us
  blocking collectives  58.7 us (62%)
  matrix products  14.3 us (15%)
  other arithmetic  8.73 us (9%)
  starting transfers between devices  6.34 us (7%)
  local copies, waits for them, and re-layouts  4.17 us (4%)
  between operations  1.57 us (2%)
    psum x1, blocking collectives, shards(): counts = lax.psum(local_counts, ('dp', 'tgt'))  33.1 us
    unnamed x1, blocking collectives  11.1 us
    all_to_all x1, blocking collectives, shards(): lax.all_to_all(raw_owner.reshape(owner_count, CAP), 'dp', split_axis=0, c...  7.9 us
    all_gather x1, blocking collectives, shards(): row_piece = lax.all_gather(owner_rows, 'tgt', axis=0, tiled=True)  6.5 us
    all_to_all x1, starting transfers between devices, shards(): lax.all_to_all(outgoing.reshape(owner_count, CAP, -1), 'dp', split_axis=0...  6.34 us
    dot_general x1, matrix products, shards(): jnp.einsum('esr,esd->erd', per_example(rank_down, examples), per_example(...  3.33 us
    dot_general x1, matrix products, shards(): jnp.einsum('esd,esr->edr', per_example(wide_hidden, examples), per_exampl...  3.31 us
    dot_general x1, matrix products, contracted_row_sums(): lax.dot_general(row_block, col_block, (((1,), (1,)), ((), ())), preferred...  2.97 us
  transfers between devices with their start and end apart: 1, of which 0 were waited for; matrix products, arithmetic and copies ran while one was open for 5% of the time, Pallas kernels for 0%

commit v1 on v0

--- a/solution.py
+++ b/solution.py
@@ -109,7 +109,20 @@
     own_targets = targets[0]
     target_inv = inverse_norms(own_targets)
     offset = lax.axis_index("tgt") * own_targets.shape[0]
-    row_piece = lax.all_gather(owner_rows, "tgt", axis=0, tiled=True)
+
+    def links_rest(sample, along_axis="tgt"):
+        nodes = jax.lax.axis_size(along_axis)
+        buffer = [sample]
+        for q in [*range(nodes - 1)]:
+            p_next = jax.lax.ppermute(
+                buffer[-1], along_axis, [(h, (h + 1) % nodes) for h in range(nodes)]
+            )
+            buffer.append(p_next)
+        ready = jnp.concatenate(buffer[::-1], 0)
+        newest = jax.lax.axis_index(along_axis)
+        return jnp.roll(ready, (newest + 1) * sample.shape[0], 0)
+
+    row_piece = links_rest(owner_rows)
     partials = task_terms(row_piece, inverse_norms(row_piece), own_targets, target_inv, offset)
     task_sums = lax.psum_scatter(partials, "tgt", scatter_dimension=0, tiled=True)
     raw_owner = jnp.max(task_sums / (TGT // TASKS), axis=1)

time: 94.3 us -> 96.8 us (1.027)
  starting transfers between devices: 6.34 us -> 0.06 us
  waiting for transfers between devices: 0.01 us -> 6.06 us
  blocking collectives: 58.7 us -> 62.4 us
    all_to_all x0 -> x1, blocking collectives: none -> 12.2 us  [shards(): lax.all_to_all(outgoing.reshape(owner_count, CAP, -1), 'dp', split_axis=0...]
    all_gather x1 -> x0, blocking collectives: 6.5 us -> none  [shards(): row_piece = lax.all_gather(owner_rows, 'tgt', axis=0, tiled=True)]
    all_to_all x1 -> x0, starting transfers between devices: 6.34 us -> none  [shards(): lax.all_to_all(outgoing.reshape(owner_count, CAP, -1), 'dp', split_axis=0...]
    ppermute x0 -> x3, waiting for transfers between devices: none -> 6.06 us  [links_rest(): jax.lax.ppermute(buffer[-1], along_axis, [(h, (h + 1) % nodes) for h in r...]
    unnamed x1, blocking collectives: 11.1 us -> 10.1 us
    psum x1, blocking collectives: 33.1 us -> 32.1 us  [shards(): counts = lax.psum(local_counts, ('dp', 'tgt'))]
  transfers between devices with their start and end apart: 1 -> 3, of which waited for: 0 -> 2; matrix products, arithmetic and copies ran while one was open for 5% -> 4% of each run, Pallas kernels for 0% -> 0%
where the time goes in v1:
time: 96.8 us; the launch traced here: 96.3 us
  blocking collectives  62.4 us (64%)
  matrix products  14.2 us (15%)
  other arithmetic  8.29 us (9%)
  waiting for transfers between devices  6.06 us (6%)
  local copies, waits for them, and re-layouts  3.62 us (4%)
  between operations  1.67 us (2%)
    psum x1, blocking collectives, shards(): counts = lax.psum(local_counts, ('dp', 'tgt'))  32.1 us
    all_to_all x1, blocking collectives, shards(): lax.all_to_all(outgoing.reshape(owner_count, CAP, -1), 'dp', split_axis=0...  12.2 us
    unnamed x1, blocking collectives  10.1 us
    all_to_all x1, blocking collectives, shards(): lax.all_to_all(raw_owner.reshape(owner_count, CAP), 'dp', split_axis=0, c...  7.9 us
    ppermute x3, waiting for transfers between devices, links_rest(): jax.lax.ppermute(buffer[-1], along_axis, [(h, (h + 1) % nodes) for h in r...  6.06 us
    dot_general x1, matrix products, shards(): jnp.einsum('esr,esd->erd', per_example(rank_down, examples), per_example(...  3.33 us
    dot_general x1, matrix products, shards(): jnp.einsum('esd,esr->edr', per_example(wide_hidden, examples), per_exampl...  3.31 us
    dot_general x1, matrix products, contracted_row_sums(): lax.dot_general(row_block, col_block, (((1,), (1,)), ((), ())), preferred...  2.97 us
  transfers between devices with their start and end apart: 3, of which 2 were waited for; matrix products, arithmetic and copies ran while one was open for 4% of the time, Pallas kernels for 0%

profile of v1, /device:TPU:0, one launch (start us, length us, event | category | flops | bytes accessed | tf_op | source)
XLA Modules:
  0.0 96.3 jit_solution(10175566040631744503)
XLA Ops:
  0.8 0.7 compare_and_fusion.1
  1.4 0.9 select_reduce_fusion.1
  2.3 0.2 convert_reduce_fusion.1
  2.5 0.7 compare_and_fusion
  3.2 2.3 %fusion.15 = bf16[192,8]{0,1:T(8,128)(2,1)S(1)} fusion(bf16[64,8]{0,1:T(8,128)(2,1)} %param.16, bf16[192,4096]{1,0:T(8,128)(2,1)} %param.12, bf16[64,4096]{1,0:T(8,128)(2,1)} %param.14), kind=kOutput, calls=%fused_computation.17 | convolution fusion | flops 100873728 | bytes 2101248 | tf_op jit(solution)/shard_map/dot_general | solution.py:74
  5.5 0.1 reshape.70
  5.6 3.3 %convolution_convert_fusion.1 = bf16[24,512,8]{1,2,0:T(8,128)(2,1)S(1)} fusion(bf16[192,4096]{1,0:T(8,128)(2,1)S(1)} %copy-done, bf16[4096,512]{1,0:T(8,128)(2,1)} %param.15, bf16[24,8,8]{1,0,2:T(8,128)(2,1)S(1)} %reshape.70), kind=kOutput, calls=%fused_computation.4 | convolution fusion | flops 807075840 | bytes 5966848 | tf_op jit(solution)/shard_map/esd,esr->edr/dot_general | solution.py:83
  8.9 0.8 copy.25
  9.8 0.3 copy.26
  10.1 1.9 %fusion.16 = bf16[192,8]{0,1:T(8,128)(2,1)S(1)} fusion(bf16[64,8]{0,1:T(8,128)(2,1)S(1)} %copy-done.2, bf16[192,4096]{1,0:T(8,128)(2,1)S(1)} %copy-done, bf16[4096,64]{0,1:T(8,128)(2,1)} %param.13), kind=kOutput, calls=%fused_computation.18 | convolution fusion | flops 100873728 | bytes 2101248 | tf_op jit(solution)/shard_map/dot_general | solution.py:71
  12.0 0.7 reshape.66
  12.8 3.3 %convolution_convert_fusion.3 = bf16[24,8,512]{2,1,0:T(8,128)(2,1)S(1)} fusion(bf16[192,4096]{1,0:T(8,128)(2,1)S(1)} %copy-done.1, bf16[4096,512]{1,0:T(8,128)(2,1)} %param.15, bf16[24,8,8]{1,0,2:T(8,128)(2,1)} %reshape.66), kind=kOutput, calls=%fused_computation.6 | convolution fusion | flops 807075840 | bytes 5966848 | tf_op jit(solution)/shard_map/esr,esd->erd/dot_general | solution.py:77
  16.2 0.2 convolution_convert_fusion
  16.4 0.1 reshape.72
  16.5 12.2 %all_to_all.14 = bf16[4,2,8192]{2,1,0:T(2,128)(2,1)S(1)} all-to-all(bf16[4,2,8192]{2,1,0:T(2,128)(2,1)S(1)} %reshape.72), channel_id=1, replica_groups=mesh['groups'=2,'dp'=4,'tgt'=4] {'dp'}, dimensions={0} | all-to-all | bytes 262144 | tf_op jit(solution)/shard_map/all_to_all | solution.py:105
  28.9 2.6 %multiply_reduce_fusion = f32[192]{0:T(256)S(1)} fusion(bf16[1,192,8192]{2,1,0:T(8,128)(2,1)} %param.17), kind=kLoop, calls=%fused_computation.1 | loop fusion | flops 4718400 | bytes 3146496 | tf_op jit(solution)/shard_map/reduce_sum | solution.py:22
  31.5 1.8 %collective-permute-done = bf16[8,8192]{1,0:T(8,128)(2,1)S(1)} collective-permute-done((bf16[8,8192]{1,0:T(8,128)(2,1)S(1)}, bf16[8,8192]{1,0:T(8,128)(2,1)S(1)}, u32[]{:S(2)}, u32[]{:S(2)}) %collective-permute-start) | collective-permute-done | bytes 131104 | tf_op jit(solution)/shard_map/ppermute | solution.py:117
  33.2 0.1 convert_reduce_fusion
  33.3 4.3 %collective-permute-done.1 = bf16[8,8192]{1,0:T(8,128)(2,1)S(1)} collective-permute-done((bf16[8,8192]{1,0:T(8,128)(2,1)S(1)}, bf16[8,8192]{1,0:T(8,128)(2,1)S(1)}, u32[]{:S(2)}, u32[]{:S(2)}) %collective-permute-start.1) | collective-permute-done | bytes 131104 | tf_op jit(solution)/shard_map/ppermute | solution.py:117
  37.7 0.6 dynamic-slice
  38.9 32.1 %psum.7 = f32[32]{0:T(128)S(1)} all-reduce(f32[32]{0:T(128)S(1)} %convert_reduce_fusion), channel_id=1, replica_groups=mesh['groups'=2,'dp'=4,'tgt'=4] {'dp','tgt'}, use_global_device_ids=true, to_apply=%region_8.9 | all-reduce | flops 32 | bytes 256 | tf_op jit(solution)/shard_map/psum | solution.py:60
  71.0 0.7 reduce_sum.78
  71.7 0.2 select_reduce_fusion
  72.0 0.2 multiply_reduce_fusion.1
  72.3 3.0 %fusion.10 = f32[32,192]{1,0:T(8,128)S(1)} fusion(bf16[1,192,8192]{2,1,0:T(8,128)(2,1)} %param.17, bf16[64,8192]{1,0:T(8,128)(2,1)S(1)} %constant_dynamic-update-slice_fusion, s32[]{:T(128)S(6)} %select_n.40, f32[192]{0:T(256)S(1)} %add_rsqrt_fusion, f32[32]{0:T(128)S(1)} %rsqrt_multiply_fusion), kind=kOutput, calls=%fused_computation.14 | convolution fusion | flops 100681728 | bytes 3696132 | tf_op jit(solution)/shard_map/dot_general | solution.py:15
  75.3 0.2 fusion.21
  75.5 10.1 %all-reduce = f32[32,16]{1,0:T(8,128)S(1)} all-reduce(f32[32,16]{1,0:T(8,128)S(1)} %fusion.21), channel_id=2, replica_groups=mesh['groups'=2,'dp'=4,'tgt'=4] {'tgt'}, use_global_device_ids=true, to_apply=%region_4.5.clone | all-reduce | flops 512 | bytes 4096
  85.6 0.1 fusion.28
  85.8 7.9 %all_to_all.15 = f32[4,1,2]{2,1,0:T(1,128)S(1)} all-to-all(f32[4,1,2]{2,1,0:T(1,128)S(1)} %bitcast.44), channel_id=1, replica_groups=mesh['groups'=2,'dp'=4,'tgt'=4] {'dp'}, dimensions={0} | all-to-all | bytes 64 | tf_op jit(solution)/shard_map/all_to_all | solution.py:129
  93.7 0.5 broadcast.77
  94.3 0.7 reduce.3
  95.1 1.2 %multiply_select_fusion = f32[24]{0:T(128)} fusion(pred[24]{0:T(512)(128)(4,1)S(1)} %compare_and_fusion, f32[24]{0:T(128)S(1)} %select_reduce_fusion.2, f32[24]{0:T(128)S(1)} %select_reduce_fusion, f32[]{:T(128)} %reduce_sum.78), kind=kLoop, calls=%fused_computation.57 | loop fusion | flops 120 | bytes 316 | tf_op jit(solution)/shard_map/jit(_where)/select_n | solution.py:135
  (31 shorter events, 0.6 us)
Async XLA Ops:
  0.0 5.6 %copy-start = (bf16[192,4096]{1,0:T(8,128)(2,1)S(1)}, bf16[192,4096]{1,0:T(8,128)(2,1)}, u32[]{:S(2)}) copy-start(bf16[192,4096]{1,0:T(8,128)(2,1)} %param.11) | copy-start | bytes 4718596
  8.9 1.2 %copy-start.2 = (bf16[64,8]{0,1:T(8,128)(2,1)S(1)}, bf16[64,8]{0,1:T(8,128)(2,1)}, u32[]{:S(2)}) copy-start(bf16[64,8]{0,1:T(8,128)(2,1)} %param.16) | copy-start | bytes 3076
  10.1 2.7 %copy-start.1 = (bf16[192,4096]{1,0:T(8,128)(2,1)S(1)}, bf16[192,4096]{1,0:T(8,128)(2,1)}, u32[]{:S(2)}) copy-start(bf16[192,4096]{1,0:T(8,128)(2,1)} %param.12) | copy-start | bytes 4718596
  28.8 4.5 %copy-start.3 = (s32[24]{0:T(128)S(1)}, s32[24]{0:T(128)}, u32[]{:S(2)}) copy-start(s32[24]{0:T(128)} %param.18) | copy-start | bytes 292
  28.8 8.9 %copy-start.4 = (u32[32]{0:T(128)S(1)}, u32[32]{0:T(128)}, u32[]{:S(2)}) copy-start(u32[32]{0:T(128)} %constant.68) | copy-start | bytes 388
  28.8 4.4 %collective-permute-start = (bf16[8,8192]{1,0:T(8,128)(2,1)S(1)}, bf16[8,8192]{1,0:T(8,128)(2,1)S(1)}, u32[]{:S(2)}, u32[]{:S(2)}) collective-permute-start(bf16[8,8192]{1,0:T(8,128)(2,1)S(1)} %reshape.73), channel_id=1, source_target_pairs={{0,1},{1,2},{2,3},{3,0},{4,5},{5,6},{6,7},{7,4},{8,9},{9,10},{10,1... | collective-permute-start | bytes 393224 | tf_op jit(solution)/shard_map/ppermute | solution.py:117
  33.2 4.4 %collective-permute-start.1 = (bf16[8,8192]{1,0:T(8,128)(2,1)S(1)}, bf16[8,8192]{1,0:T(8,128)(2,1)S(1)}, u32[]{:S(2)}, u32[]{:S(2)}) collective-permute-start(bf16[8,8192]{1,0:T(8,128)(2,1)S(1)} %collective-permute-done), channel_id=1, source_target_pairs={{0,1},{1,2},{2,3},{3,0},{4,5},{5,6},{6,7},{7,4},{8,9},{9,10},{10,1... | collective-permute-start | bytes 393224 | tf_op jit(solution)/shard_map/ppermute | solution.py:117
  37.6 34.3 %collective-permute-start.2 = (bf16[8,8192]{1,0:T(8,128)(2,1)S(1)}, bf16[8,8192]{1,0:T(8,128)(2,1)S(1)}, u32[]{:S(2)}, u32[]{:S(2)}) collective-permute-start(bf16[8,8192]{1,0:T(8,128)(2,1)S(1)} %collective-permute-done.1), channel_id=1, source_target_pairs={{0,1},{1,2},{2,3},{3,0},{4,5},{5,6},{6,7},{7,4},{8,9},{9,10},{10,1... | collective-permute-start | bytes 393224 | tf_op jit(solution)/shard_map/ppermute | solution.py:117
